TPU v7x, 256 devices: a whole 4x4x8 slice. The times are simulated.
256 devices in a mesh: rows: 64 (over z, x, core), coil: 4 (over y).
Axes of the slice: x: 4, y: 4, z: 8, core: 2. Of those that a mesh axis runs over, the one named last changes fastest.
Arguments:
- kspace: float32 [128, 32768], P('coil', 'rows'), may hold values from -6 to 6
- sample_mask: int32 [128, 32768], P('coil', 'rows'), may hold values 0 or 1
- start_basis: float32 [4, 2048, 128], P('coil', 'rows'), may hold values from -6 to 6
Outputs:
- recovered: float32 [128, 32768], P('coil', 'rows')
- basis: float32 [4, 2048, 128], P('coil', 'rows')
All inputs are finite; a program needn't handle non-finite values. No bound on the sum of `sample_mask` on one device may be relied on, other than what follows from the above.
Results may differ from a plain program's by a relative error of at most 0.00011.
Values sent between devices are 32-bit elements; how exact they have to be, the bound alone decides.
A program may use at most 64 MiB of HBM per device.

v0:
```python
import jax
import jax.numpy as jnp
from jax import lax
from jax.sharding import PartitionSpec as P

KER = 64
ITERS = 2
threshold = 0.05


def shifted(block, axis, distance):
    devices = range(lax.axis_size(axis))
    route = [((i - distance) % len(devices), i) for i in devices]
    return lax.ppermute(block, axis, route)


def orthonormal(normal_rows, gram_matrix):
    factor = jnp.linalg.cholesky(gram_matrix)
    return lax.linalg.triangular_solve(
        factor, normal_rows, left_side=False, lower=True, transpose_a=True
    )


def coil_total(partial_value):
    return lax.psum(partial_value, "coil")


def shards(kspace, sample_mask, start_basis):
    highest = lax.Precision.HIGHEST
    channels = kspace.shape[0]
    tile_rows = kspace.shape[1]
    mask_float = sample_mask.astype(jnp.float32)
    sampled = kspace * mask_float
    next_rim = shifted(sampled[:, : KER - 1], "rows", -1)
    extended = jnp.concatenate([sampled, next_rim], axis=1)
    hankel_cols = jnp.stack(
        [extended[:, offset : offset + tile_rows] for offset in range(KER)], axis=0
    )
    hankel_cols = hankel_cols.reshape(KER * channels, tile_rows)
    owned_basis = start_basis.reshape(start_basis.shape[1], start_basis.shape[2])

    def fold_basis(shard_piece):
        return lax.dot_general(
            shard_piece,
            hankel_cols,
            (((0,), (0,)), ((), ())),
            precision=highest,
            preferred_element_type=jnp.float32,
        )

    def apply_hankel(current):
        partial_value = fold_basis(lax.all_gather(current, "rows", axis=0, tiled=True))
        return coil_total(partial_value)

    for iteration in range(ITERS):
        images = apply_hankel(owned_basis)
        normal_rows = lax.psum_scatter(
            lax.dot_general(
                hankel_cols,
                images,
                (((1,), (1,)), ((), ())),
                precision=highest,
                preferred_element_type=jnp.float32,
            ),
            "rows",
            scatter_dimension=0,
            tiled=True,
        )
        local_gram = jnp.dot(
            normal_rows.T, normal_rows, precision=highest, preferred_element_type=jnp.float32
        )
        gram_matrix = lax.psum(local_gram, ("rows", "coil"))
        owned_basis = orthonormal(normal_rows, gram_matrix)
    images = apply_hankel(owned_basis)
    projected = jnp.dot(
        lax.all_gather(owned_basis, "rows", axis=0, tiled=True),
        images,
        precision=highest,
        preferred_element_type=jnp.float32,
    )
    stacked = projected.reshape(KER, channels, tile_rows)
    spread = jnp.zeros((channels, tile_rows + KER - 1), jnp.float32)
    for offset in range(KER):
        spread = spread.at[:, offset : offset + tile_rows].add(stacked[offset])
    carried = shifted(spread[:, tile_rows:], "rows", 1)
    estimate = spread[:, :tile_rows].at[:, : KER - 1].add(carried) / KER
    residual = mask_float * (kspace - estimate)
    recovered = estimate + residual - jnp.clip(residual, -threshold, threshold)
    return (recovered, owned_basis.reshape(1, owned_basis.shape[0], owned_basis.shape[1]))


def solution(mesh):
    return jax.shard_map(
        shards,
        mesh=mesh,
        in_specs=(P("coil", "rows"), P("coil", "rows"), P("coil", "rows", None)),
        out_specs=(P("coil", "rows"), P("coil", "rows", None)),
        check_vma=False,
    )
```

profile of v0, /device:TPU:16, one launch (start us, length us, event | category | flops | bytes accessed | tf_op | source)
XLA Modules:
  0.0 1392.1 jit_solution(3663720347566413571)
XLA Ops:
  8.7 7.5 collective-permute-start
  62.2 28.1 %all-gather.9.cloned.1.call-done = f32[1,2048,128]{2,1,0:T(8,128)} async-done(((f32[1,32,128]{2,1,0:T(8,128)}), f32[1,2048,128]{2,1,0:T(8,128)}) %all-gather.9.cloned.1.call-update) | async-done | bytes 1048592 | tf_op jit(solution)/shard_map/all_gather | solution.py:52
  90.4 9.9 convolution_bitcast_fusion
  100.5 43.9 %all-reduce.7.cloned.1.call-done = f32[128,512]{0,1:T(8,128)} async-done(((f32[128,512]{0,1:T(8,128)}), f32[128,512]{0,1:T(8,128)}) %all-reduce.7.cloned.1.call-update) | async-done | bytes 262160 | tf_op jit(solution)/shard_map/psum | solution.py:25
  144.4 6.6 fusion.135
  151.0 141.7 %reduce-scatter.3.cloned.1.call-done = f32[32,128]{1,0:T(8,128)} async-done(((f32[2048,128]{1,0:T(8,128)}), f32[32,128]{1,0:T(8,128)}) %reduce-scatter.3.cloned.1.call-update) | async-done | bytes 16400 | tf_op jit(solution)/shard_map/reduce_scatter | solution.py:57
  292.7 1.7 fusion.136
  294.5 243.0 %all-reduce.9.cloned.1.call-done = f32[128,128]{0,1:T(8,128)} async-done(((f32[128,128]{0,1:T(8,128)}), f32[128,128]{0,1:T(8,128)}) %all-reduce.9.cloned.1.call-update) | async-done | bytes 65552 | tf_op jit(solution)/shard_map/psum | solution.py:72
  539.3 11.7 cholesky.44
  552.3 9.8 custom-call.6
  563.9 74.0 %all-gather.5.cloned.1.call-done = f32[2048,128]{1,0:T(8,128)} async-done(((f32[32,128]{1,0:T(8,128)}), f32[2048,128]{1,0:T(8,128)}) %all-gather.5.cloned.1.call-update) | async-done | bytes 1048592 | tf_op jit(solution)/shard_map/all_gather | solution.py:52
  637.9 5.8 fusion.137
  643.8 44.0 %all-reduce.11.cloned.1.call-done = f32[128,512]{1,0:T(8,128)} async-done(((f32[128,512]{1,0:T(8,128)}), f32[128,512]{1,0:T(8,128)}) %all-reduce.11.cloned.1.call-update) | async-done | bytes 262160 | tf_op jit(solution)/shard_map/psum | solution.py:25
  687.9 6.6 fusion.138
  694.6 141.7 %reduce-scatter.5.cloned.1.call-done = f32[32,128]{1,0:T(8,128)} async-done(((f32[2048,128]{1,0:T(8,128)}), f32[32,128]{1,0:T(8,128)}) %reduce-scatter.5.cloned.1.call-update) | async-done | bytes 16400 | tf_op jit(solution)/shard_map/reduce_scatter | solution.py:57
  836.3 1.7 fusion.139
  838.5 242.7 %all-reduce.13.cloned.1.call-done = f32[128,128]{0,1:T(8,128)} async-done(((f32[128,128]{0,1:T(8,128)}), f32[128,128]{0,1:T(8,128)}) %all-reduce.13.cloned.1.call-update) | async-done | bytes 65552 | tf_op jit(solution)/shard_map/psum | solution.py:72
  1083.0 11.7 cholesky.55
  1096.0 9.8 custom-call.7
  1107.4 74.2 %all-gather.7.cloned.1.call-done = f32[2048,128]{1,0:T(8,128)} async-done(((f32[32,128]{1,0:T(8,128)}), f32[2048,128]{1,0:T(8,128)}) %all-gather.7.cloned.1.call-update) | async-done | bytes 1048592 | tf_op jit(solution)/shard_map/all_gather | solution.py:76
  1181.6 5.9 fusion.140
  1230.1 1.6 all-reduce.15.cloned.1.call-done
  1231.7 4.5 fusion.141
  1241.0 1.6 add_select_fusion.59
  1252.1 1.6 add_select_fusion.54
  1256.6 1.6 add_select_fusion.52
  1261.1 1.6 add_select_fusion.50
  1265.6 1.6 add_select_fusion.48
  1274.5 1.6 add_select_fusion.44
  1279.1 1.6 add_select_fusion.42
  1281.4 1.6 add_select_fusion.41
  1294.9 1.6 add_select_fusion.35
  1299.4 1.6 add_select_fusion.33
  1301.7 1.6 add_select_fusion.32
  1304.0 1.6 add_select_fusion.31
  1308.4 1.6 add_select_fusion.29
  1312.9 1.6 add_select_fusion.27
  1319.6 1.6 add_select_fusion.24
  1321.9 1.6 add_select_fusion.23
  1330.9 1.6 add_select_fusion.19
  1339.8 1.6 add_select_fusion.15
  1348.7 1.6 add_select_fusion.11
  1353.1 1.6 add_select_fusion.9
  1359.8 1.6 add_select_fusion.6
  1364.3 1.6 add_select_fusion.4
  1369.1 1.6 add_select_fusion.2
  1371.3 1.6 add_select_fusion.1
  1378.1 5.2 collective-permute-done.1
  (280 shorter events, 205.0 us)
Async XLA Ops:
  7.2 83.2 %all-gather.9.cloned.1.call-start = ((), (), s32[]{:S(2)}) async-start(), calls=%async_computation.11 | async-start | bytes 1064960 | tf_op jit(solution)/shard_map/all_gather | solution.py:52
  8.7 8.9 collective-permute-start
  16.2 128.1 %all-reduce.7.cloned.1.call-start = ((), (), s32[]{:S(2)}) async-start(), calls=%async_computation.2 | async-start | bytes 524288 | tf_op jit(solution)/shard_map/psum | solution.py:25
  100.3 192.4 %reduce-scatter.3.cloned.1.call-start = ((), (), s32[]{:S(2)}) async-start(), calls=%async_computation.3 | async-start | bytes 1064960 | tf_op jit(solution)/shard_map/reduce_scatter | solution.py:57
  151.0 386.5 %all-reduce.9.cloned.1.call-start = ((), (), s32[]{:S(2)}) async-start(), calls=%async_computation.4 | async-start | bytes 131072 | tf_op jit(solution)/shard_map/psum | solution.py:72
  294.4 343.5 %all-gather.5.cloned.1.call-start = ((), (), s32[]{:S(2)}) async-start(), calls=%async_computation.5 | async-start | bytes 1064960 | tf_op jit(solution)/shard_map/all_gather | solution.py:52
  563.7 124.2 %all-reduce.11.cloned.1.call-start = ((), (), s32[]{:S(2)}) async-start(), calls=%async_computation.6 | async-start | bytes 524288 | tf_op jit(solution)/shard_map/psum | solution.py:25
  643.8 192.5 %reduce-scatter.5.cloned.1.call-start = ((), (), s32[]{:S(2)}) async-start(), calls=%async_computation.7 | async-start | bytes 1064960 | tf_op jit(solution)/shard_map/reduce_scatter | solution.py:57
  694.5 386.7 %all-reduce.13.cloned.1.call-start = ((), (), s32[]{:S(2)}) async-start(), calls=%async_computation.8 | async-start | bytes 131072 | tf_op jit(solution)/shard_map/psum | solution.py:72
  838.0 343.6 %all-gather.7.cloned.1.call-start = ((), (), s32[]{:S(2)}) async-start(), calls=%async_computation.9 | async-start | bytes 1064960 | tf_op jit(solution)/shard_map/all_gather | solution.py:76
  1107.4 124.3 %all-reduce.15.cloned.1.call-start = ((), (), s32[]{:S(2)}) async-start(), calls=%async_computation.10 | async-start | bytes 524288 | tf_op jit(solution)/shard_map/psum | solution.py:25
  1181.6 50.0 %copy-start.1 = (f32[2048,128]{1,0:T(8,128)S(1)}, f32[2048,128]{1,0:T(8,128)}, u32[]{:S(2)}) copy-start(f32[2048,128]{1,0:T(8,128)} %all-gather.7.cloned.1.call-done) | copy-start | bytes 3145732
  1236.1 2.0 copy-start
  1321.9 62.4 %copy-start.2 = (f32[32,512]{1,0:T(8,128)S(1)}, f32[32,512]{1,0:T(8,128)}, u32[]{:S(2)}) copy-start(f32[32,512]{1,0:T(8,128)} %param.136) | copy-start | bytes 196612
  1321.9 62.4 %copy-start.3 = (s32[32,512]{1,0:T(8,128)S(1)}, s32[32,512]{1,0:T(8,128)}, u32[]{:S(2)}) copy-start(s32[32,512]{1,0:T(8,128)} %param.137) | copy-start | bytes 196612
  1376.8 6.5 collective-permute-start.1
Sparse Core Ops, SparseCore 0:
  16.4 73.9 all-gather.8
  100.4 43.9 all-reduce.6
  151.1 141.5 reduce-scatter.2
  298.6 238.8 all-reduce.8
  563.8 74.1 all-gather.4
  643.9 43.9 all-reduce.10
  694.6 141.5 reduce-scatter.4
  842.3 238.8 all-reduce.12
  1107.5 74.1 all-gather.6
  1187.7 43.9 all-reduce.14
where the time goes:
time: 1400 us; the launch traced here: 1390 us
  waiting for transfers between devices  1040 us (74%)
  other arithmetic  234 us (17%)
  local copies, waits for them, and re-layouts  46 us (3%)
  matrix products  45.7 us (3%)
  between operations  15.6 us (1%)
    psum x2, waiting for transfers between devices, shards(): gram_matrix = lax.psum(local_gram, ('rows', 'coil'))  486 us
    reduce_scatter x2, waiting for transfers between devices, shards(): lax.psum_scatter(lax.dot_general(hankel_cols, images, (((1,), (1,)), ((),...  283 us
    another operation x128, other arithmetic  139 us
    all_gather x2, waiting for transfers between devices, apply_hankel(): lax.all_gather(current, 'rows', axis=0, tiled=True)  102 us
    psum x3, waiting for transfers between devices, coil_total(): return lax.psum(partial_value, 'coil')  89.5 us
    all_gather x1, waiting for transfers between devices, shards(): lax.all_gather(owned_basis, 'rows', axis=0, tiled=True)  74.2 us
    unnamed x63, other arithmetic  45.3 us
    scatter-add x64, local copies, waits for them, and re-layouts, shards(): spread = spread.at[:, offset:offset + tile_rows].add(stacked[offset])  43.2 us
  transfers between devices with their start and end apart: 12, of which 12 were waited for; matrix products, arithmetic and copies ran while one was open for 6% of the time, Pallas kernels for 0%

commit v1 on v0

--- a/solution.py
+++ b/solution.py
@@ -69,7 +69,7 @@
         local_gram = jnp.dot(
             normal_rows.T, normal_rows, precision=highest, preferred_element_type=jnp.float32
         )
-        gram_matrix = lax.psum(local_gram, ("rows", "coil"))
+        gram_matrix = lax.psum(lax.psum(local_gram, "rows"), "coil")
         owned_basis = orthonormal(normal_rows, gram_matrix)
     images = apply_hankel(owned_basis)
     projected = jnp.dot(

time: 1400 us -> 1360 us (0.971)
  waiting for transfers between devices: 1040 us -> 995 us
    psum x2 -> x4, waiting for transfers between devices: 486 us -> 431 us  [shards(): gram_matrix = lax.psum(lax.psum(local_gram, 'rows'), 'coil')]
  transfers between devices with their start and end apart: 12 -> 14, of which waited for: 12 -> 14; matrix products, arithmetic and copies ran while one was open for 6% -> 7% of each run, Pallas kernels for 0% -> 0%
where the time goes in v1:
time: 1360 us; the launch traced here: 1350 us
  waiting for transfers between devices  995 us (73%)
  other arithmetic  234 us (17%)
  local copies, waits for them, and re-layouts  46 us (3%)
  matrix products  45.7 us (3%)
  between operations  15.7 us (1%)
    psum x4, waiting for transfers between devices, shards(): gram_matrix = lax.psum(lax.psum(local_gram, 'rows'), 'coil')  431 us
    reduce_scatter x2, waiting for transfers between devices, shards(): lax.psum_scatter(lax.dot_general(hankel_cols, images, (((1,), (1,)), ((),...  283 us
    another operation x128, other arithmetic  139 us
    all_gather x2, waiting for transfers between devices, apply_hankel(): lax.all_gather(current, 'rows', axis=0, tiled=True)  106 us
    psum x3, waiting for transfers between devices, coil_total(): return lax.psum(partial_value, 'coil')  89.5 us
    all_gather x1, waiting for transfers between devices, shards(): lax.all_gather(owned_basis, 'rows', axis=0, tiled=True)  78.2 us
    unnamed x63, other arithmetic  45.3 us
    scatter-add x64, local copies, waits for them, and re-layouts, shards(): spread = spread.at[:, offset:offset + tile_rows].add(stacked[offset])  43.2 us
  transfers between devices with their start and end apart: 14, of which 14 were waited for; matrix products, arithmetic and copies ran while one was open for 7% of the time, Pallas kernels for 0%

profile of v1, /device:TPU:16, one launch (start us, length us, event | category | flops | bytes accessed | tf_op | source)
XLA Modules:
  0.0 1345.2 jit_solution(13047322408078931624)
XLA Ops:
  8.7 7.5 collective-permute-start
  62.2 28.1 %all-gather.9.cloned.1.call-done = f32[1,2048,128]{2,1,0:T(8,128)} async-done(((f32[1,32,128]{2,1,0:T(8,128)}), f32[1,2048,128]{2,1,0:T(8,128)}) %all-gather.9.cloned.1.call-update) | async-done | bytes 1048592 | tf_op jit(solution)/shard_map/all_gather | solution.py:52
  90.4 9.9 convolution_bitcast_fusion
  100.5 43.9 %all-reduce.9.cloned.1.call-done = f32[128,512]{0,1:T(8,128)} async-done(((f32[128,512]{0,1:T(8,128)}), f32[128,512]{0,1:T(8,128)}) %all-reduce.9.cloned.1.call-update) | async-done | bytes 262160 | tf_op jit(solution)/shard_map/psum | solution.py:25
  144.4 6.6 fusion.135
  151.0 141.7 %reduce-scatter.3.cloned.1.call-done = f32[32,128]{1,0:T(8,128)} async-done(((f32[2048,128]{1,0:T(8,128)}), f32[32,128]{1,0:T(8,128)}) %reduce-scatter.3.cloned.1.call-update) | async-done | bytes 16400 | tf_op jit(solution)/shard_map/reduce_scatter | solution.py:57
  292.7 1.7 fusion.136
  294.5 170.9 %all-reduce.11.cloned.1.call-done = f32[128,128]{0,1:T(8,128)} async-done(((f32[128,128]{0,1:T(8,128)}), f32[128,128]{0,1:T(8,128)}) %all-reduce.11.cloned.1.call-update) | async-done | bytes 65552 | tf_op jit(solution)/shard_map/psum | solution.py:72
  465.5 44.6 %all-reduce.13.cloned.1.call-done = f32[128,128]{0,1:T(8,128)} async-done(((f32[128,128]{0,1:T(8,128)}), f32[128,128]{0,1:T(8,128)}) %all-reduce.13.cloned.1.call-update) | async-done | bytes 65552 | tf_op jit(solution)/shard_map/psum | solution.py:72
  511.9 11.7 cholesky.44
  524.9 9.8 custom-call.6
  536.5 77.9 %all-gather.5.cloned.1.call-done = f32[2048,128]{1,0:T(8,128)} async-done(((f32[32,128]{1,0:T(8,128)}), f32[2048,128]{1,0:T(8,128)}) %all-gather.5.cloned.1.call-update) | async-done | bytes 1048592 | tf_op jit(solution)/shard_map/all_gather | solution.py:52
  614.5 5.8 fusion.137
  620.4 44.0 %all-reduce.15.cloned.1.call-done = f32[128,512]{1,0:T(8,128)} async-done(((f32[128,512]{1,0:T(8,128)}), f32[128,512]{1,0:T(8,128)}) %all-reduce.15.cloned.1.call-update) | async-done | bytes 262160 | tf_op jit(solution)/shard_map/psum | solution.py:25
  664.4 6.6 fusion.138
  671.1 141.7 %reduce-scatter.5.cloned.1.call-done = f32[32,128]{1,0:T(8,128)} async-done(((f32[2048,128]{1,0:T(8,128)}), f32[32,128]{1,0:T(8,128)}) %reduce-scatter.5.cloned.1.call-update) | async-done | bytes 16400 | tf_op jit(solution)/shard_map/reduce_scatter | solution.py:57
  812.8 1.7 fusion.139
  814.6 171.1 %all-reduce.17.cloned.1.call-done = f32[128,128]{0,1:T(8,128)} async-done(((f32[128,128]{0,1:T(8,128)}), f32[128,128]{0,1:T(8,128)}) %all-reduce.17.cloned.1.call-update) | async-done | bytes 65552 | tf_op jit(solution)/shard_map/psum | solution.py:72
  986.2 44.2 %all-reduce.19.cloned.1.call-done = f32[128,128]{0,1:T(8,128)} async-done(((f32[128,128]{0,1:T(8,128)}), f32[128,128]{0,1:T(8,128)}) %all-reduce.19.cloned.1.call-update) | async-done | bytes 65552 | tf_op jit(solution)/shard_map/psum | solution.py:72
  1032.1 11.7 cholesky.55
  1045.2 9.8 custom-call.7
  1056.6 78.2 %all-gather.7.cloned.1.call-done = f32[2048,128]{1,0:T(8,128)} async-done(((f32[32,128]{1,0:T(8,128)}), f32[2048,128]{1,0:T(8,128)}) %all-gather.7.cloned.1.call-update) | async-done | bytes 1048592 | tf_op jit(solution)/shard_map/all_gather | solution.py:76
  1134.7 5.9 fusion.140
  1183.2 1.6 all-reduce.21.cloned.1.call-done
  1184.8 4.5 fusion.141
  1194.1 1.6 add_select_fusion.59
  1205.2 1.6 add_select_fusion.54
  1209.7 1.6 add_select_fusion.52
  1218.7 1.6 add_select_fusion.48
  1227.6 1.6 add_select_fusion.44
  1232.2 1.6 add_select_fusion.42
  1234.5 1.6 add_select_fusion.41
  1248.0 1.6 add_select_fusion.35
  1252.5 1.6 add_select_fusion.33
  1254.8 1.6 add_select_fusion.32
  1261.5 1.6 add_select_fusion.29
  1266.0 1.6 add_select_fusion.27
  1272.7 1.6 add_select_fusion.24
  1275.0 1.6 add_select_fusion.23
  1284.0 1.6 add_select_fusion.19
  1292.9 1.6 add_select_fusion.15
  1301.8 1.6 add_select_fusion.11
  1306.2 1.6 add_select_fusion.9
  1312.9 1.6 add_select_fusion.6
  1317.4 1.6 add_select_fusion.4
  1322.2 1.6 add_select_fusion.2
  1324.4 1.6 add_select_fusion.1
  1331.2 5.2 collective-permute-done.1
  (286 shorter events, 208.3 us)
Async XLA Ops:
  7.2 83.2 %all-gather.9.cloned.1.call-start = ((), (), s32[]{:S(2)}) async-start(), calls=%async_computation.13 | async-start | bytes 1064960 | tf_op jit(solution)/shard_map/all_gather | solution.py:52
  8.7 8.9 collective-permute-start
  16.2 128.1 %all-reduce.9.cloned.1.call-start = ((), (), s32[]{:S(2)}) async-start(), calls=%async_computation.2 | async-start | bytes 524288 | tf_op jit(solution)/shard_map/psum | solution.py:25
  100.3 192.4 %reduce-scatter.3.cloned.1.call-start = ((), (), s32[]{:S(2)}) async-start(), calls=%async_computation.3 | async-start | bytes 1064960 | tf_op jit(solution)/shard_map/reduce_scatter | solution.py:57
  151.0 314.4 %all-reduce.11.cloned.1.call-start = ((), (), s32[]{:S(2)}) async-start(), calls=%async_computation.4 | async-start | bytes 131072 | tf_op jit(solution)/shard_map/psum | solution.py:72
  294.4 215.6 %all-reduce.13.cloned.1.call-start = ((), (), s32[]{:S(2)}) async-start(), calls=%async_computation.5 | async-start | bytes 131072 | tf_op jit(solution)/shard_map/psum | solution.py:72
  465.5 149.0 %all-gather.5.cloned.1.call-start = ((), (), s32[]{:S(2)}) async-start(), calls=%async_computation.6 | async-start | bytes 1064960 | tf_op jit(solution)/shard_map/all_gather | solution.py:52
  536.3 128.1 %all-reduce.15.cloned.1.call-start = ((), (), s32[]{:S(2)}) async-start(), calls=%async_computation.7 | async-start | bytes 524288 | tf_op jit(solution)/shard_map/psum | solution.py:25
  620.3 192.5 %reduce-scatter.5.cloned.1.call-start = ((), (), s32[]{:S(2)}) async-start(), calls=%async_computation.8 | async-start | bytes 1064960 | tf_op jit(solution)/shard_map/reduce_scatter | solution.py:57
  671.0 314.6 %all-reduce.17.cloned.1.call-start = ((), (), s32[]{:S(2)}) async-start(), calls=%async_computation.9 | async-start | bytes 131072 | tf_op jit(solution)/shard_map/psum | solution.py:72
  814.5 215.8 %all-reduce.19.cloned.1.call-start = ((), (), s32[]{:S(2)}) async-start(), calls=%async_computation.10 | async-start | bytes 131072 | tf_op jit(solution)/shard_map/psum | solution.py:72
  985.7 149.0 %all-gather.7.cloned.1.call-start = ((), (), s32[]{:S(2)}) async-start(), calls=%async_computation.11 | async-start | bytes 1064960 | tf_op jit(solution)/shard_map/all_gather | solution.py:76
  1056.5 128.2 %all-reduce.21.cloned.1.call-start = ((), (), s32[]{:S(2)}) async-start(), calls=%async_computation.12 | async-start | bytes 524288 | tf_op jit(solution)/shard_map/psum | solution.py:25
  1134.7 50.0 %copy-start.1 = (f32[2048,128]{1,0:T(8,128)S(1)}, f32[2048,128]{1,0:T(8,128)}, u32[]{:S(2)}) copy-start(f32[2048,128]{1,0:T(8,128)} %all-gather.7.cloned.1.call-done) | copy-start | bytes 3145732
  1189.2 2.0 copy-start
  1275.0 62.4 %copy-start.2 = (f32[32,512]{1,0:T(8,128)S(1)}, f32[32,512]{1,0:T(8,128)}, u32[]{:S(2)}) copy-start(f32[32,512]{1,0:T(8,128)} %param.136) | copy-start | bytes 196612
  1275.0 62.4 %copy-start.3 = (s32[32,512]{1,0:T(8,128)S(1)}, s32[32,512]{1,0:T(8,128)}, u32[]{:S(2)}) copy-start(s32[32,512]{1,0:T(8,128)} %param.137) | copy-start | bytes 196612
  1329.9 6.5 collective-permute-start.1
Sparse Core Ops, SparseCore 0:
  16.4 73.9 all-gather.8
  100.4 43.9 all-reduce.8
  151.1 141.5 reduce-scatter.2
  296.6 168.7 all-reduce.10
  467.6 42.4 all-reduce.12
  536.4 78.0 all-gather.4
  620.4 43.9 all-reduce.14
  671.2 141.5 reduce-scatter.4
  816.8 168.8 all-reduce.16
  987.8 42.4 all-reduce.18
  1056.6 78.0 all-gather.6
  1140.8 43.9 all-reduce.20
